TPU v7x, 512 devices: a whole 4x8x8 slice. The times are simulated.
512 devices in a mesh: wide: 64 (over y, z_lo, core), rep: 8 (over z_hi, x).
Axes of the slice: x: 4, y: 8, z: 8 (z_hi: 2, z_lo: 4; z = z_hi * 4 + z_lo), core: 2. Of those that a mesh axis runs over, the one named last changes fastest.
Arguments:
- features: bfloat16 [65536, 512], P(('wide', 'rep')), may hold values from -6 to 6
- w_query: bfloat16 [512, 512], replicated, may hold values from -0.25 to 0.25
- w_key: bfloat16 [512, 512], replicated, may hold values from -0.25 to 0.25
- w_out: bfloat16 [512, 512], replicated, may hold values from -0.25 to 0.25
- edge_weight: bfloat16 [64, 8, 96, 128, 128], P('wide', 'rep'), may hold values from -0.23925781 to 0.23925781
- tile_slot: int32 [64, 8, 96], P('wide', 'rep'), may hold values from 0 to 511, as said below
- tile_count: int32 [64, 8], P('wide', 'rep'), may hold values from 1 to 96, as said below
Outputs:
- updated: bfloat16 [65536, 512], P(('wide', 'rep'))
Inputs may be any that keep to these rules, and one draw needn't show every extreme that they name: For each w and r the first tile_count[w, r] entries of tile_slot[w, r] are distinct and ascending; all 96 entries of a list are distinct. `tile_count`: some device has 96 live tiles.
All inputs are finite; a program needn't handle non-finite values.
Results may differ from a plain program's by a relative error of at most 0.014.
Values may be sent and summed in bfloat16 or wider, within the bound.
A program may use at most 64 MiB of HBM per device.

v0:
```python
import jax
import jax.numpy as jnp
from jax import lax
from jax.sharding import PartitionSpec as P


def from_behind(block, axis, distance):
    devices = range(lax.axis_size(axis))
    route = [((i - distance) % len(devices), i) for i in devices]
    return lax.ppermute(block, axis, route)


def on_device(features, w_query, w_key, w_out, edge_weight, tile_slot, tile_count):
    tile_rows = features.shape[0]
    feat_width = features.shape[1]
    n_wide = lax.axis_size("wide")
    n_rep = lax.axis_size("rep")
    query_rows = jnp.dot(features, w_query, preferred_element_type=jnp.float32).astype(jnp.bfloat16)
    key_rows = jnp.dot(features, w_key, preferred_element_type=jnp.float32).astype(jnp.bfloat16)
    receivers = lax.all_gather(query_rows, "rep", axis=0, tiled=True)
    tile_slots = tile_slot[0, 0]
    live_count = tile_count[0, 0]
    weights = edge_weight[0, 0]
    step_of = tile_slots // n_rep
    active = jnp.arange(tile_slots.shape[0], dtype=jnp.int32) < live_count
    below = step_of[None, :] < jnp.arange(n_wide + 1, dtype=jnp.int32)[:, None]
    bounds = jnp.sum((active[None, :] & below).astype(jnp.int32), axis=1)
    factor = 1.0 / float(feat_width) ** 0.5

    def one_tile(tile_num, sender, partial_value):
        block = tile_slots[tile_num] % n_rep
        targets = lax.dynamic_slice_in_dim(receivers, block * tile_rows, tile_rows, 0)
        scores = (
            lax.dot_general(
                targets, sender, (((1,), (1,)), ((), ())), preferred_element_type=jnp.float32
            )
            * factor
        )
        weighted = (jnp.tanh(scores) * weights[tile_num].astype(jnp.float32)).astype(jnp.bfloat16)
        contrib = jnp.dot(weighted, sender, preferred_element_type=jnp.float32)
        previous = lax.dynamic_slice_in_dim(partial_value, block * tile_rows, tile_rows, 0)
        return lax.dynamic_update_slice_in_dim(
            partial_value, previous + contrib, block * tile_rows, 0
        )

    def one_step(step_num, sender, partial_value):
        return lax.fori_loop(
            bounds[step_num],
            bounds[step_num + 1],
            lambda tile_num, acc: one_tile(tile_num, sender, acc),
            partial_value,
        )

    partial_value = jnp.zeros((n_rep * tile_rows, feat_width), jnp.float32)
    partial_value = one_step(0, key_rows, partial_value)

    def advance(step_num, state_pair):
        sender = from_behind(state_pair[0], "wide", 1)
        return (sender, one_step(step_num, sender, state_pair[1]))

    partial_value = lax.fori_loop(1, n_wide, advance, (key_rows, partial_value))[1]
    summed = lax.psum_scatter(
        partial_value.astype(jnp.bfloat16), "rep", scatter_dimension=0, tiled=True
    )
    mixed = features.astype(jnp.float32) + jnp.dot(
        summed, w_out, preferred_element_type=jnp.float32
    )
    return mixed.astype(jnp.bfloat16)


def solution(mesh):
    in_specs = (
        P(("wide", "rep"), None),
        P(),
        P(),
        P(),
        P("wide", "rep", None, None, None),
        P("wide", "rep", None),
        P("wide", "rep"),
    )
    out_specs = P(("wide", "rep"), None)
    return jax.shard_map(
        on_device, mesh=mesh, in_specs=in_specs, out_specs=out_specs, check_vma=False
    )
```

profile of v0, /device:TPU:8, one launch (start us, length us, event | category | flops | bytes accessed | tf_op | source)
XLA Modules:
  0.0 2005.7 jit_solution(4528999640472336238)
XLA Ops:
  12.8 69.9 %all-gather.2.cloned.1.call-done = bf16[1024,512]{1,0:T(8,128)(2,1)} async-done(((bf16[128,512]{1,0:T(8,128)(2,1)}), bf16[1024,512]{1,0:T(8,128)(2,1)}) %all-gather.2.cloned.1.call-update) | async-done | bytes 1048592 | tf_op jit(solution)/shard_map/all_gather | solution.py:20
  92.7 1685.8 %while.66 = (s32[]{:T(128)}, bf16[128,512]{1,0:T(8,128)(2,1)S(1)}, f32[1024,512]{1,0:T(8,128)S(1)}, s32[65]{0:T(128)S(1)}, s32[96]{0:T(128)S(1)}, /*index=5*/bf1...) while((s32[]{:T(128)}, bf16[128,512]{1,0:T(8,128)(2,1)S(1)}, ...), condition=%wide.region_6.7_spmd, body=%wide.region_3.6_spmd.sunk | while | flops 33685532 | bytes 1739011 | solution.py:61
  177.3 26.8 %collective-permute-start = (bf16[128,512]{1,0:T(8,128)(2,1)S(1)}, bf16[128,512]{1,0:T(8,128)(2,1)S(1)}, u32[]{:S(2)}, u32[]{:S(2)}) collective-permute-start(bf16[128,512]{1,0:T(8,128)(2,1)S(1)} %get-tuple-element.784), channel_id=1, source_target_pairs={{504,0},{0,8},{8,16},{16,24},{24,32},{32,40},{40,48},{48,56},{56,6... | collective-permute-start | bytes 393224 | tf_op jit(solution)/shard_map/while/body/eval_jaxpr/ppermute | solution.py:10
  216.5 27.7 %collective-permute-start = (bf16[128,512]{1,0:T(8,128)(2,1)S(1)}, bf16[128,512]{1,0:T(8,128)(2,1)S(1)}, u32[]{:S(2)}, u32[]{:S(2)}) collective-permute-start(bf16[128,512]{1,0:T(8,128)(2,1)S(1)} %get-tuple-element.784), channel_id=1, source_target_pairs={{504,0},{0,8},{8,16},{16,24},{24,32},{32,40},{40,48},{48,56},{56,6... | collective-permute-start | bytes 393224 | tf_op jit(solution)/shard_map/while/body/eval_jaxpr/ppermute | solution.py:10
  368.7 22.0 %collective-permute-start = (bf16[128,512]{1,0:T(8,128)(2,1)S(1)}, bf16[128,512]{1,0:T(8,128)(2,1)S(1)}, u32[]{:S(2)}, u32[]{:S(2)}) collective-permute-start(bf16[128,512]{1,0:T(8,128)(2,1)S(1)} %get-tuple-element.784), channel_id=1, source_target_pairs={{504,0},{0,8},{8,16},{16,24},{24,32},{32,40},{40,48},{48,56},{56,6... | collective-permute-start | bytes 393224 | tf_op jit(solution)/shard_map/while/body/eval_jaxpr/ppermute | solution.py:10
  393.0 22.0 %collective-permute-start = (bf16[128,512]{1,0:T(8,128)(2,1)S(1)}, bf16[128,512]{1,0:T(8,128)(2,1)S(1)}, u32[]{:S(2)}, u32[]{:S(2)}) collective-permute-start(bf16[128,512]{1,0:T(8,128)(2,1)S(1)} %get-tuple-element.784), channel_id=1, source_target_pairs={{504,0},{0,8},{8,16},{16,24},{24,32},{32,40},{40,48},{48,56},{56,6... | collective-permute-start | bytes 393224 | tf_op jit(solution)/shard_map/while/body/eval_jaxpr/ppermute | solution.py:10
  453.3 40.4 %collective-permute-done = bf16[128,512]{1,0:T(8,128)(2,1)S(1)} collective-permute-done((bf16[128,512]{1,0:T(8,128)(2,1)S(1)}, bf16[128,512]{1,0:T(8,128)(2,1)S(1)}, u32[]{:S(2)}, u32[]{:S(2)}) %collective-permute-start) | collective-permute-done | bytes 131104 | tf_op jit(solution)/shard_map/while/body/eval_jaxpr/ppermute | solution.py:10
  497.6 28.8 %collective-permute-done = bf16[128,512]{1,0:T(8,128)(2,1)S(1)} collective-permute-done((bf16[128,512]{1,0:T(8,128)(2,1)S(1)}, bf16[128,512]{1,0:T(8,128)(2,1)S(1)}, u32[]{:S(2)}, u32[]{:S(2)}) %collective-permute-start) | collective-permute-done | bytes 131104 | tf_op jit(solution)/shard_map/while/body/eval_jaxpr/ppermute | solution.py:10
  546.0 37.2 %collective-permute-done = bf16[128,512]{1,0:T(8,128)(2,1)S(1)} collective-permute-done((bf16[128,512]{1,0:T(8,128)(2,1)S(1)}, bf16[128,512]{1,0:T(8,128)(2,1)S(1)}, u32[]{:S(2)}, u32[]{:S(2)}) %collective-permute-start) | collective-permute-done | bytes 131104 | tf_op jit(solution)/shard_map/while/body/eval_jaxpr/ppermute | solution.py:10
  658.6 22.0 %collective-permute-start = (bf16[128,512]{1,0:T(8,128)(2,1)S(1)}, bf16[128,512]{1,0:T(8,128)(2,1)S(1)}, u32[]{:S(2)}, u32[]{:S(2)}) collective-permute-start(bf16[128,512]{1,0:T(8,128)(2,1)S(1)} %get-tuple-element.784), channel_id=1, source_target_pairs={{504,0},{0,8},{8,16},{16,24},{24,32},{32,40},{40,48},{48,56},{56,6... | collective-permute-start | bytes 393224 | tf_op jit(solution)/shard_map/while/body/eval_jaxpr/ppermute | solution.py:10
  681.2 33.0 %collective-permute-done = bf16[128,512]{1,0:T(8,128)(2,1)S(1)} collective-permute-done((bf16[128,512]{1,0:T(8,128)(2,1)S(1)}, bf16[128,512]{1,0:T(8,128)(2,1)S(1)}, u32[]{:S(2)}, u32[]{:S(2)}) %collective-permute-start) | collective-permute-done | bytes 131104 | tf_op jit(solution)/shard_map/while/body/eval_jaxpr/ppermute | solution.py:10
  763.5 48.6 %collective-permute-done = bf16[128,512]{1,0:T(8,128)(2,1)S(1)} collective-permute-done((bf16[128,512]{1,0:T(8,128)(2,1)S(1)}, bf16[128,512]{1,0:T(8,128)(2,1)S(1)}, u32[]{:S(2)}, u32[]{:S(2)}) %collective-permute-start) | collective-permute-done | bytes 131104 | tf_op jit(solution)/shard_map/while/body/eval_jaxpr/ppermute | solution.py:10
  853.5 30.2 %collective-permute-done = bf16[128,512]{1,0:T(8,128)(2,1)S(1)} collective-permute-done((bf16[128,512]{1,0:T(8,128)(2,1)S(1)}, bf16[128,512]{1,0:T(8,128)(2,1)S(1)}, u32[]{:S(2)}, u32[]{:S(2)}) %collective-permute-start) | collective-permute-done | bytes 131104 | tf_op jit(solution)/shard_map/while/body/eval_jaxpr/ppermute | solution.py:10
  897.7 36.4 %collective-permute-done = bf16[128,512]{1,0:T(8,128)(2,1)S(1)} collective-permute-done((bf16[128,512]{1,0:T(8,128)(2,1)S(1)}, bf16[128,512]{1,0:T(8,128)(2,1)S(1)}, u32[]{:S(2)}, u32[]{:S(2)}) %collective-permute-start) | collective-permute-done | bytes 131104 | tf_op jit(solution)/shard_map/while/body/eval_jaxpr/ppermute | solution.py:10
  935.4 22.6 %collective-permute-start = (bf16[128,512]{1,0:T(8,128)(2,1)S(1)}, bf16[128,512]{1,0:T(8,128)(2,1)S(1)}, u32[]{:S(2)}, u32[]{:S(2)}) collective-permute-start(bf16[128,512]{1,0:T(8,128)(2,1)S(1)} %get-tuple-element.784), channel_id=1, source_target_pairs={{504,0},{0,8},{8,16},{16,24},{24,32},{32,40},{40,48},{48,56},{56,6... | collective-permute-start | bytes 393224 | tf_op jit(solution)/shard_map/while/body/eval_jaxpr/ppermute | solution.py:10
  963.7 45.6 %collective-permute-done = bf16[128,512]{1,0:T(8,128)(2,1)S(1)} collective-permute-done((bf16[128,512]{1,0:T(8,128)(2,1)S(1)}, bf16[128,512]{1,0:T(8,128)(2,1)S(1)}, u32[]{:S(2)}, u32[]{:S(2)}) %collective-permute-start) | collective-permute-done | bytes 131104 | tf_op jit(solution)/shard_map/while/body/eval_jaxpr/ppermute | solution.py:10
  1253.9 68.2 %collective-permute-done = bf16[128,512]{1,0:T(8,128)(2,1)S(1)} collective-permute-done((bf16[128,512]{1,0:T(8,128)(2,1)S(1)}, bf16[128,512]{1,0:T(8,128)(2,1)S(1)}, u32[]{:S(2)}, u32[]{:S(2)}) %collective-permute-start) | collective-permute-done | bytes 131104 | tf_op jit(solution)/shard_map/while/body/eval_jaxpr/ppermute | solution.py:10
  1441.4 21.4 %collective-permute-done = bf16[128,512]{1,0:T(8,128)(2,1)S(1)} collective-permute-done((bf16[128,512]{1,0:T(8,128)(2,1)S(1)}, bf16[128,512]{1,0:T(8,128)(2,1)S(1)}, u32[]{:S(2)}, u32[]{:S(2)}) %collective-permute-start) | collective-permute-done | bytes 131104 | tf_op jit(solution)/shard_map/while/body/eval_jaxpr/ppermute | solution.py:10
  1473.4 27.9 %collective-permute-done = bf16[128,512]{1,0:T(8,128)(2,1)S(1)} collective-permute-done((bf16[128,512]{1,0:T(8,128)(2,1)S(1)}, bf16[128,512]{1,0:T(8,128)(2,1)S(1)}, u32[]{:S(2)}, u32[]{:S(2)}) %collective-permute-start) | collective-permute-done | bytes 131104 | tf_op jit(solution)/shard_map/while/body/eval_jaxpr/ppermute | solution.py:10
  1513.5 32.7 %collective-permute-done = bf16[128,512]{1,0:T(8,128)(2,1)S(1)} collective-permute-done((bf16[128,512]{1,0:T(8,128)(2,1)S(1)}, bf16[128,512]{1,0:T(8,128)(2,1)S(1)}, u32[]{:S(2)}, u32[]{:S(2)}) %collective-permute-start) | collective-permute-done | bytes 131104 | tf_op jit(solution)/shard_map/while/body/eval_jaxpr/ppermute | solution.py:10
  1558.4 41.1 %collective-permute-done = bf16[128,512]{1,0:T(8,128)(2,1)S(1)} collective-permute-done((bf16[128,512]{1,0:T(8,128)(2,1)S(1)}, bf16[128,512]{1,0:T(8,128)(2,1)S(1)}, u32[]{:S(2)}, u32[]{:S(2)}) %collective-permute-start) | collective-permute-done | bytes 131104 | tf_op jit(solution)/shard_map/while/body/eval_jaxpr/ppermute | solution.py:10
  1645.3 42.3 %collective-permute-done = bf16[128,512]{1,0:T(8,128)(2,1)S(1)} collective-permute-done((bf16[128,512]{1,0:T(8,128)(2,1)S(1)}, bf16[128,512]{1,0:T(8,128)(2,1)S(1)}, u32[]{:S(2)}, u32[]{:S(2)}) %collective-permute-start) | collective-permute-done | bytes 131104 | tf_op jit(solution)/shard_map/while/body/eval_jaxpr/ppermute | solution.py:10
  1699.7 37.2 %collective-permute-done = bf16[128,512]{1,0:T(8,128)(2,1)S(1)} collective-permute-done((bf16[128,512]{1,0:T(8,128)(2,1)S(1)}, bf16[128,512]{1,0:T(8,128)(2,1)S(1)}, u32[]{:S(2)}, u32[]{:S(2)}) %collective-permute-start) | collective-permute-done | bytes 131104 | tf_op jit(solution)/shard_map/while/body/eval_jaxpr/ppermute | solution.py:10
  1779.7 217.4 %reduce-scatter.2.cloned.1.call-done = bf16[128,512]{1,0:T(8,128)(2,1)} async-done(((bf16[1024,512]{1,0:T(8,128)(2,1)}), bf16[128,512]{1,0:T(8,128)(2,1)}) %reduce-scatter.2.cloned.1.call-update) | async-done | bytes 131088 | tf_op jit(solution)/shard_map/reduce_scatter | solution.py:62
  (364 shorter events, 1034.0 us)
Async XLA Ops:
  6.5 76.2 %all-gather.2.cloned.1.call-start = ((), (), s32[]{:S(2)}) async-start(), calls=%async_computation.1 | async-start | bytes 1179648 | tf_op jit(solution)/shard_map/all_gather | solution.py:20
  9.4 1987.6 %reduce-scatter.2.cloned.1.call-start = ((), (), s32[]{:S(2)}) async-start(), calls=%async_computation.2 | async-start | bytes 1179648 | tf_op jit(solution)/shard_map/reduce_scatter | solution.py:62
  177.3 27.7 %collective-permute-start = (bf16[128,512]{1,0:T(8,128)(2,1)S(1)}, bf16[128,512]{1,0:T(8,128)(2,1)S(1)}, u32[]{:S(2)}, u32[]{:S(2)}) collective-permute-start(bf16[128,512]{1,0:T(8,128)(2,1)S(1)} %get-tuple-element.784), channel_id=1, source_target_pairs={{504,0},{0,8},{8,16},{16,24},{24,32},{32,40},{40,48},{48,56},{56,6... | collective-permute-start | bytes 393224 | tf_op jit(solution)/shard_map/while/body/eval_jaxpr/ppermute | solution.py:10
  216.5 28.6 %collective-permute-start = (bf16[128,512]{1,0:T(8,128)(2,1)S(1)}, bf16[128,512]{1,0:T(8,128)(2,1)S(1)}, u32[]{:S(2)}, u32[]{:S(2)}) collective-permute-start(bf16[128,512]{1,0:T(8,128)(2,1)S(1)} %get-tuple-element.784), channel_id=1, source_target_pairs={{504,0},{0,8},{8,16},{16,24},{24,32},{32,40},{40,48},{48,56},{56,6... | collective-permute-start | bytes 393224 | tf_op jit(solution)/shard_map/while/body/eval_jaxpr/ppermute | solution.py:10
  299.9 23.0 %collective-permute-start = (bf16[128,512]{1,0:T(8,128)(2,1)S(1)}, bf16[128,512]{1,0:T(8,128)(2,1)S(1)}, u32[]{:S(2)}, u32[]{:S(2)}) collective-permute-start(bf16[128,512]{1,0:T(8,128)(2,1)S(1)} %get-tuple-element.784), channel_id=1, source_target_pairs={{504,0},{0,8},{8,16},{16,24},{24,32},{32,40},{40,48},{48,56},{56,6... | collective-permute-start | bytes 393224 | tf_op jit(solution)/shard_map/while/body/eval_jaxpr/ppermute | solution.py:10
  393.0 27.8 %collective-permute-start = (bf16[128,512]{1,0:T(8,128)(2,1)S(1)}, bf16[128,512]{1,0:T(8,128)(2,1)S(1)}, u32[]{:S(2)}, u32[]{:S(2)}) collective-permute-start(bf16[128,512]{1,0:T(8,128)(2,1)S(1)} %get-tuple-element.784), channel_id=1, source_target_pairs={{504,0},{0,8},{8,16},{16,24},{24,32},{32,40},{40,48},{48,56},{56,6... | collective-permute-start | bytes 393224 | tf_op jit(solution)/shard_map/while/body/eval_jaxpr/ppermute | solution.py:10
  446.3 47.5 %collective-permute-start = (bf16[128,512]{1,0:T(8,128)(2,1)S(1)}, bf16[128,512]{1,0:T(8,128)(2,1)S(1)}, u32[]{:S(2)}, u32[]{:S(2)}) collective-permute-start(bf16[128,512]{1,0:T(8,128)(2,1)S(1)} %get-tuple-element.784), channel_id=1, source_target_pairs={{504,0},{0,8},{8,16},{16,24},{24,32},{32,40},{40,48},{48,56},{56,6... | collective-permute-start | bytes 393224 | tf_op jit(solution)/shard_map/while/body/eval_jaxpr/ppermute | solution.py:10
  495.0 31.3 %collective-permute-start = (bf16[128,512]{1,0:T(8,128)(2,1)S(1)}, bf16[128,512]{1,0:T(8,128)(2,1)S(1)}, u32[]{:S(2)}, u32[]{:S(2)}) collective-permute-start(bf16[128,512]{1,0:T(8,128)(2,1)S(1)} %get-tuple-element.784), channel_id=1, source_target_pairs={{504,0},{0,8},{8,16},{16,24},{24,32},{32,40},{40,48},{48,56},{56,6... | collective-permute-start | bytes 393224 | tf_op jit(solution)/shard_map/while/body/eval_jaxpr/ppermute | solution.py:10
  543.5 39.7 %collective-permute-start = (bf16[128,512]{1,0:T(8,128)(2,1)S(1)}, bf16[128,512]{1,0:T(8,128)(2,1)S(1)}, u32[]{:S(2)}, u32[]{:S(2)}) collective-permute-start(bf16[128,512]{1,0:T(8,128)(2,1)S(1)} %get-tuple-element.784), channel_id=1, source_target_pairs={{504,0},{0,8},{8,16},{16,24},{24,32},{32,40},{40,48},{48,56},{56,6... | collective-permute-start | bytes 393224 | tf_op jit(solution)/shard_map/while/body/eval_jaxpr/ppermute | solution.py:10
  658.6 55.6 %collective-permute-start = (bf16[128,512]{1,0:T(8,128)(2,1)S(1)}, bf16[128,512]{1,0:T(8,128)(2,1)S(1)}, u32[]{:S(2)}, u32[]{:S(2)}) collective-permute-start(bf16[128,512]{1,0:T(8,128)(2,1)S(1)} %get-tuple-element.784), channel_id=1, source_target_pairs={{504,0},{0,8},{8,16},{16,24},{24,32},{32,40},{40,48},{48,56},{56,6... | collective-permute-start | bytes 393224 | tf_op jit(solution)/shard_map/while/body/eval_jaxpr/ppermute | solution.py:10
  755.6 56.4 %collective-permute-start = (bf16[128,512]{1,0:T(8,128)(2,1)S(1)}, bf16[128,512]{1,0:T(8,128)(2,1)S(1)}, u32[]{:S(2)}, u32[]{:S(2)}) collective-permute-start(bf16[128,512]{1,0:T(8,128)(2,1)S(1)} %get-tuple-element.784), channel_id=1, source_target_pairs={{504,0},{0,8},{8,16},{16,24},{24,32},{32,40},{40,48},{48,56},{56,6... | collective-permute-start | bytes 393224 | tf_op jit(solution)/shard_map/while/body/eval_jaxpr/ppermute | solution.py:10
  851.0 32.7 %collective-permute-start = (bf16[128,512]{1,0:T(8,128)(2,1)S(1)}, bf16[128,512]{1,0:T(8,128)(2,1)S(1)}, u32[]{:S(2)}, u32[]{:S(2)}) collective-permute-start(bf16[128,512]{1,0:T(8,128)(2,1)S(1)} %get-tuple-element.784), channel_id=1, source_target_pairs={{504,0},{0,8},{8,16},{16,24},{24,32},{32,40},{40,48},{48,56},{56,6... | collective-permute-start | bytes 393224 | tf_op jit(solution)/shard_map/while/body/eval_jaxpr/ppermute | solution.py:10
  895.2 38.9 %collective-permute-start = (bf16[128,512]{1,0:T(8,128)(2,1)S(1)}, bf16[128,512]{1,0:T(8,128)(2,1)S(1)}, u32[]{:S(2)}, u32[]{:S(2)}) collective-permute-start(bf16[128,512]{1,0:T(8,128)(2,1)S(1)} %get-tuple-element.784), channel_id=1, source_target_pairs={{504,0},{0,8},{8,16},{16,24},{24,32},{32,40},{40,48},{48,56},{56,6... | collective-permute-start | bytes 393224 | tf_op jit(solution)/shard_map/while/body/eval_jaxpr/ppermute | solution.py:10
  935.4 23.5 %collective-permute-start = (bf16[128,512]{1,0:T(8,128)(2,1)S(1)}, bf16[128,512]{1,0:T(8,128)(2,1)S(1)}, u32[]{:S(2)}, u32[]{:S(2)}) collective-permute-start(bf16[128,512]{1,0:T(8,128)(2,1)S(1)} %get-tuple-element.784), channel_id=1, source_target_pairs={{504,0},{0,8},{8,16},{16,24},{24,32},{32,40},{40,48},{48,56},{56,6... | collective-permute-start | bytes 393224 | tf_op jit(solution)/shard_map/while/body/eval_jaxpr/ppermute | solution.py:10
  960.2 49.1 %collective-permute-start = (bf16[128,512]{1,0:T(8,128)(2,1)S(1)}, bf16[128,512]{1,0:T(8,128)(2,1)S(1)}, u32[]{:S(2)}, u32[]{:S(2)}) collective-permute-start(bf16[128,512]{1,0:T(8,128)(2,1)S(1)} %get-tuple-element.784), channel_id=1, source_target_pairs={{504,0},{0,8},{8,16},{16,24},{24,32},{32,40},{40,48},{48,56},{56,6... | collective-permute-start | bytes 393224 | tf_op jit(solution)/shard_map/while/body/eval_jaxpr/ppermute | solution.py:10
  1010.5 23.0 %collective-permute-start = (bf16[128,512]{1,0:T(8,128)(2,1)S(1)}, bf16[128,512]{1,0:T(8,128)(2,1)S(1)}, u32[]{:S(2)}, u32[]{:S(2)}) collective-permute-start(bf16[128,512]{1,0:T(8,128)(2,1)S(1)} %get-tuple-element.784), channel_id=1, source_target_pairs={{504,0},{0,8},{8,16},{16,24},{24,32},{32,40},{40,48},{48,56},{56,6... | collective-permute-start | bytes 393224 | tf_op jit(solution)/shard_map/while/body/eval_jaxpr/ppermute | solution.py:10
  1168.4 28.9 %collective-permute-start = (bf16[128,512]{1,0:T(8,128)(2,1)S(1)}, bf16[128,512]{1,0:T(8,128)(2,1)S(1)}, u32[]{:S(2)}, u32[]{:S(2)}) collective-permute-start(bf16[128,512]{1,0:T(8,128)(2,1)S(1)} %get-tuple-element.784), channel_id=1, source_target_pairs={{504,0},{0,8},{8,16},{16,24},{24,32},{32,40},{40,48},{48,56},{56,6... | collective-permute-start | bytes 393224 | tf_op jit(solution)/shard_map/while/body/eval_jaxpr/ppermute | solution.py:10
  1251.4 70.7 %collective-permute-start = (bf16[128,512]{1,0:T(8,128)(2,1)S(1)}, bf16[128,512]{1,0:T(8,128)(2,1)S(1)}, u32[]{:S(2)}, u32[]{:S(2)}) collective-permute-start(bf16[128,512]{1,0:T(8,128)(2,1)S(1)} %get-tuple-element.784), channel_id=1, source_target_pairs={{504,0},{0,8},{8,16},{16,24},{24,32},{32,40},{40,48},{48,56},{56,6... | collective-permute-start | bytes 393224 | tf_op jit(solution)/shard_map/while/body/eval_jaxpr/ppermute | solution.py:10
  1438.9 23.9 %collective-permute-start = (bf16[128,512]{1,0:T(8,128)(2,1)S(1)}, bf16[128,512]{1,0:T(8,128)(2,1)S(1)}, u32[]{:S(2)}, u32[]{:S(2)}) collective-permute-start(bf16[128,512]{1,0:T(8,128)(2,1)S(1)} %get-tuple-element.784), channel_id=1, source_target_pairs={{504,0},{0,8},{8,16},{16,24},{24,32},{32,40},{40,48},{48,56},{56,6... | collective-permute-start | bytes 393224 | tf_op jit(solution)/shard_map/while/body/eval_jaxpr/ppermute | solution.py:10
  1464.1 37.3 %collective-permute-start = (bf16[128,512]{1,0:T(8,128)(2,1)S(1)}, bf16[128,512]{1,0:T(8,128)(2,1)S(1)}, u32[]{:S(2)}, u32[]{:S(2)}) collective-permute-start(bf16[128,512]{1,0:T(8,128)(2,1)S(1)} %get-tuple-element.784), channel_id=1, source_target_pairs={{504,0},{0,8},{8,16},{16,24},{24,32},{32,40},{40,48},{48,56},{56,6... | collective-permute-start | bytes 393224 | tf_op jit(solution)/shard_map/while/body/eval_jaxpr/ppermute | solution.py:10
  1511.0 35.3 %collective-permute-start = (bf16[128,512]{1,0:T(8,128)(2,1)S(1)}, bf16[128,512]{1,0:T(8,128)(2,1)S(1)}, u32[]{:S(2)}, u32[]{:S(2)}) collective-permute-start(bf16[128,512]{1,0:T(8,128)(2,1)S(1)} %get-tuple-element.784), channel_id=1, source_target_pairs={{504,0},{0,8},{8,16},{16,24},{24,32},{32,40},{40,48},{48,56},{56,6... | collective-permute-start | bytes 393224 | tf_op jit(solution)/shard_map/while/body/eval_jaxpr/ppermute | solution.py:10
  1555.8 43.6 %collective-permute-start = (bf16[128,512]{1,0:T(8,128)(2,1)S(1)}, bf16[128,512]{1,0:T(8,128)(2,1)S(1)}, u32[]{:S(2)}, u32[]{:S(2)}) collective-permute-start(bf16[128,512]{1,0:T(8,128)(2,1)S(1)} %get-tuple-element.784), channel_id=1, source_target_pairs={{504,0},{0,8},{8,16},{16,24},{24,32},{32,40},{40,48},{48,56},{56,6... | collective-permute-start | bytes 393224 | tf_op jit(solution)/shard_map/while/body/eval_jaxpr/ppermute | solution.py:10
  1642.7 44.8 %collective-permute-start = (bf16[128,512]{1,0:T(8,128)(2,1)S(1)}, bf16[128,512]{1,0:T(8,128)(2,1)S(1)}, u32[]{:S(2)}, u32[]{:S(2)}) collective-permute-start(bf16[128,512]{1,0:T(8,128)(2,1)S(1)} %get-tuple-element.784), channel_id=1, source_target_pairs={{504,0},{0,8},{8,16},{16,24},{24,32},{32,40},{40,48},{48,56},{56,6... | collective-permute-start | bytes 393224 | tf_op jit(solution)/shard_map/while/body/eval_jaxpr/ppermute | solution.py:10
  1697.2 39.7 %collective-permute-start = (bf16[128,512]{1,0:T(8,128)(2,1)S(1)}, bf16[128,512]{1,0:T(8,128)(2,1)S(1)}, u32[]{:S(2)}, u32[]{:S(2)}) collective-permute-start(bf16[128,512]{1,0:T(8,128)(2,1)S(1)} %get-tuple-element.784), channel_id=1, source_target_pairs={{504,0},{0,8},{8,16},{16,24},{24,32},{32,40},{40,48},{48,56},{56,6... | collective-permute-start | bytes 393224 | tf_op jit(solution)/shard_map/while/body/eval_jaxpr/ppermute | solution.py:10
  (45 other events, 1100.0 us)
Sparse Core Ops, SparseCore 0:
  10.5 72.1 all-gather.1
  1779.8 217.1 reduce-scatter.1
where the time goes:
time: 2020 us; the launch traced here: 2010 us
  waiting for transfers between devices  1270 us (63%)
  starting transfers between devices  392 us (19%)
  loops' own time  235 us (12%)
  local copies, waits for them, and re-layouts  55.7 us (3%)
  matrix products  35.8 us (2%)
    ppermute x63, waiting for transfers between devices, from_behind(): return lax.ppermute(block, axis, route)  984 us
    ppermute x63, starting transfers between devices, from_behind(): return lax.ppermute(block, axis, route)  392 us
    another operation x64, loops' own time, one_step(): lax.fori_loop(bounds[step_num], bounds[step_num + 1], lambda tile_num, ac...  232 us
    reduce_scatter x1, waiting for transfers between devices, on_device(): lax.psum_scatter(partial_value.astype(jnp.bfloat16), 'rep', scatter_dimen...  217 us
    all_gather x1, waiting for transfers between devices, on_device(): receivers = lax.all_gather(query_rows, 'rep', axis=0, tiled=True)  69.9 us
  transfers between devices with their start and end apart: 65, of which 65 were waited for; matrix products, arithmetic and copies ran while one was open for 2% of the time, Pallas kernels for 0%

commit v1 on v0

--- a/solution.py
+++ b/solution.py
@@ -17,7 +17,9 @@
     n_rep = lax.axis_size("rep")
     query_rows = jnp.dot(features, w_query, preferred_element_type=jnp.float32).astype(jnp.bfloat16)
     key_rows = jnp.dot(features, w_key, preferred_element_type=jnp.float32).astype(jnp.bfloat16)
-    receivers = lax.all_gather(query_rows, "rep", axis=0, tiled=True)
+    receivers = jnp.concatenate(
+        lax.all_to_all(jnp.stack([query_rows] * lax.axis_size("rep")), "rep", 0, 0), axis=0
+    )
     tile_slots = tile_slot[0, 0]
     live_count = tile_count[0, 0]
     weights = edge_weight[0, 0]

time: 2020 us -> 1910 us (0.946)
  waiting for transfers between devices: 1270 us -> 1180 us
    all_gather x1 -> x0, waiting for transfers between devices: 69.9 us -> none  [on_device(): receivers = lax.all_gather(query_rows, 'rep', axis=0, tiled=True)]
    ppermute x63, waiting for transfers between devices: 984 us -> 940 us  [from_behind(): return lax.ppermute(block, axis, route)]
    all_to_all x0 -> x1, waiting for transfers between devices: none -> 27.1 us  [on_device(): lax.all_to_all(jnp.stack([query_rows] * lax.axis_size('rep')), 'rep', 0, 0)]
where the time goes in v1:
time: 1910 us; the launch traced here: 1900 us
  waiting for transfers between devices  1180 us (62%)
  starting transfers between devices  399 us (21%)
  loops' own time  220 us (12%)
  local copies, waits for them, and re-layouts  57.6 us (3%)
  matrix products  34 us (2%)
    ppermute x63, waiting for transfers between devices, from_behind(): return lax.ppermute(block, axis, route)  940 us
    ppermute x63, starting transfers between devices, from_behind(): return lax.ppermute(block, axis, route)  386 us
    another operation x64, loops' own time, one_step(): lax.fori_loop(bounds[step_num], bounds[step_num + 1], lambda tile_num, ac...  217 us
    reduce_scatter x1, waiting for transfers between devices, on_device(): lax.psum_scatter(partial_value.astype(jnp.bfloat16), 'rep', scatter_dimen...  208 us
  transfers between devices with their start and end apart: 65, of which 65 were waited for; matrix products, arithmetic and copies ran while one was open for 2% of the time, Pallas kernels for 0%

profile of v1, /device:TPU:8, one launch (start us, length us, event | category | flops | bytes accessed | tf_op | source)
XLA Modules:
  0.0 1901.5 jit_solution(972846846424928354)
XLA Ops:
  24.2 27.1 %all-to-all-done = bf16[8,128,512]{2,1,0:T(8,128)(2,1)S(1)} async-done(((bf16[8,128,512]{2,1,0:T(8,128)(2,1)}), bf16[8,128,512]{2,1,0:T(8,128)(2,1)S(1)}, u32[]{:S(2)}, u32[]{:S(2)}) %all-to-all-start) | async-done | bytes 1048608 | tf_op jit(solution)/shard_map/all_to_all | solution.py:21
  62.0 1621.3 %while.66 = (s32[]{:T(128)}, bf16[128,512]{1,0:T(8,128)(2,1)S(1)}, f32[1024,512]{1,0:T(8,128)S(1)}, s32[65]{0:T(128)S(1)}, s32[96]{0:T(128)S(1)}, /*index=5*/bf1...) while((s32[]{:T(128)}, bf16[128,512]{1,0:T(8,128)(2,1)S(1)}, ...), condition=%wide.region_6.7_spmd, body=%wide.region_3.6_spmd.sunk | while | flops 33685532 | bytes 1739011 | solution.py:63
  144.0 26.9 %collective-permute-start = (bf16[128,512]{1,0:T(8,128)(2,1)S(1)}, bf16[128,512]{1,0:T(8,128)(2,1)S(1)}, u32[]{:S(2)}, u32[]{:S(2)}) collective-permute-start(bf16[128,512]{1,0:T(8,128)(2,1)S(1)} %get-tuple-element.784), channel_id=1, source_target_pairs={{504,0},{0,8},{8,16},{16,24},{24,32},{32,40},{40,48},{48,56},{56,6... | collective-permute-start | bytes 393224 | tf_op jit(solution)/shard_map/while/body/eval_jaxpr/ppermute | solution.py:10
  183.2 26.5 %collective-permute-start = (bf16[128,512]{1,0:T(8,128)(2,1)S(1)}, bf16[128,512]{1,0:T(8,128)(2,1)S(1)}, u32[]{:S(2)}, u32[]{:S(2)}) collective-permute-start(bf16[128,512]{1,0:T(8,128)(2,1)S(1)} %get-tuple-element.784), channel_id=1, source_target_pairs={{504,0},{0,8},{8,16},{16,24},{24,32},{32,40},{40,48},{48,56},{56,6... | collective-permute-start | bytes 393224 | tf_op jit(solution)/shard_map/while/body/eval_jaxpr/ppermute | solution.py:10
  329.7 21.2 %collective-permute-start = (bf16[128,512]{1,0:T(8,128)(2,1)S(1)}, bf16[128,512]{1,0:T(8,128)(2,1)S(1)}, u32[]{:S(2)}, u32[]{:S(2)}) collective-permute-start(bf16[128,512]{1,0:T(8,128)(2,1)S(1)} %get-tuple-element.784), channel_id=1, source_target_pairs={{504,0},{0,8},{8,16},{16,24},{24,32},{32,40},{40,48},{48,56},{56,6... | collective-permute-start | bytes 393224 | tf_op jit(solution)/shard_map/while/body/eval_jaxpr/ppermute | solution.py:10
  353.0 21.2 %collective-permute-start = (bf16[128,512]{1,0:T(8,128)(2,1)S(1)}, bf16[128,512]{1,0:T(8,128)(2,1)S(1)}, u32[]{:S(2)}, u32[]{:S(2)}) collective-permute-start(bf16[128,512]{1,0:T(8,128)(2,1)S(1)} %get-tuple-element.784), channel_id=1, source_target_pairs={{504,0},{0,8},{8,16},{16,24},{24,32},{32,40},{40,48},{48,56},{56,6... | collective-permute-start | bytes 393224 | tf_op jit(solution)/shard_map/while/body/eval_jaxpr/ppermute | solution.py:10
  411.2 37.8 %collective-permute-done = bf16[128,512]{1,0:T(8,128)(2,1)S(1)} collective-permute-done((bf16[128,512]{1,0:T(8,128)(2,1)S(1)}, bf16[128,512]{1,0:T(8,128)(2,1)S(1)}, u32[]{:S(2)}, u32[]{:S(2)}) %collective-permute-start) | collective-permute-done | bytes 131104 | tf_op jit(solution)/shard_map/while/body/eval_jaxpr/ppermute | solution.py:10
  452.7 27.6 %collective-permute-done = bf16[128,512]{1,0:T(8,128)(2,1)S(1)} collective-permute-done((bf16[128,512]{1,0:T(8,128)(2,1)S(1)}, bf16[128,512]{1,0:T(8,128)(2,1)S(1)}, u32[]{:S(2)}, u32[]{:S(2)}) %collective-permute-start) | collective-permute-done | bytes 131104 | tf_op jit(solution)/shard_map/while/body/eval_jaxpr/ppermute | solution.py:10
  499.4 35.6 %collective-permute-done = bf16[128,512]{1,0:T(8,128)(2,1)S(1)} collective-permute-done((bf16[128,512]{1,0:T(8,128)(2,1)S(1)}, bf16[128,512]{1,0:T(8,128)(2,1)S(1)}, u32[]{:S(2)}, u32[]{:S(2)}) %collective-permute-start) | collective-permute-done | bytes 131104 | tf_op jit(solution)/shard_map/while/body/eval_jaxpr/ppermute | solution.py:10
  606.8 22.0 %collective-permute-start = (bf16[128,512]{1,0:T(8,128)(2,1)S(1)}, bf16[128,512]{1,0:T(8,128)(2,1)S(1)}, u32[]{:S(2)}, u32[]{:S(2)}) collective-permute-start(bf16[128,512]{1,0:T(8,128)(2,1)S(1)} %get-tuple-element.784), channel_id=1, source_target_pairs={{504,0},{0,8},{8,16},{16,24},{24,32},{32,40},{40,48},{48,56},{56,6... | collective-permute-start | bytes 393224 | tf_op jit(solution)/shard_map/while/body/eval_jaxpr/ppermute | solution.py:10
  629.4 30.2 %collective-permute-done = bf16[128,512]{1,0:T(8,128)(2,1)S(1)} collective-permute-done((bf16[128,512]{1,0:T(8,128)(2,1)S(1)}, bf16[128,512]{1,0:T(8,128)(2,1)S(1)}, u32[]{:S(2)}, u32[]{:S(2)}) %collective-permute-start) | collective-permute-done | bytes 131104 | tf_op jit(solution)/shard_map/while/body/eval_jaxpr/ppermute | solution.py:10
  707.0 46.5 %collective-permute-done = bf16[128,512]{1,0:T(8,128)(2,1)S(1)} collective-permute-done((bf16[128,512]{1,0:T(8,128)(2,1)S(1)}, bf16[128,512]{1,0:T(8,128)(2,1)S(1)}, u32[]{:S(2)}, u32[]{:S(2)}) %collective-permute-start) | collective-permute-done | bytes 131104 | tf_op jit(solution)/shard_map/while/body/eval_jaxpr/ppermute | solution.py:10
  793.6 29.0 %collective-permute-done = bf16[128,512]{1,0:T(8,128)(2,1)S(1)} collective-permute-done((bf16[128,512]{1,0:T(8,128)(2,1)S(1)}, bf16[128,512]{1,0:T(8,128)(2,1)S(1)}, u32[]{:S(2)}, u32[]{:S(2)}) %collective-permute-start) | collective-permute-done | bytes 131104 | tf_op jit(solution)/shard_map/while/body/eval_jaxpr/ppermute | solution.py:10
  836.4 34.4 %collective-permute-done = bf16[128,512]{1,0:T(8,128)(2,1)S(1)} collective-permute-done((bf16[128,512]{1,0:T(8,128)(2,1)S(1)}, bf16[128,512]{1,0:T(8,128)(2,1)S(1)}, u32[]{:S(2)}, u32[]{:S(2)}) %collective-permute-start) | collective-permute-done | bytes 131104 | tf_op jit(solution)/shard_map/while/body/eval_jaxpr/ppermute | solution.py:10
  872.0 21.4 %collective-permute-start = (bf16[128,512]{1,0:T(8,128)(2,1)S(1)}, bf16[128,512]{1,0:T(8,128)(2,1)S(1)}, u32[]{:S(2)}, u32[]{:S(2)}) collective-permute-start(bf16[128,512]{1,0:T(8,128)(2,1)S(1)} %get-tuple-element.784), channel_id=1, source_target_pairs={{504,0},{0,8},{8,16},{16,24},{24,32},{32,40},{40,48},{48,56},{56,6... | collective-permute-start | bytes 393224 | tf_op jit(solution)/shard_map/while/body/eval_jaxpr/ppermute | solution.py:10
  899.0 44.0 %collective-permute-done = bf16[128,512]{1,0:T(8,128)(2,1)S(1)} collective-permute-done((bf16[128,512]{1,0:T(8,128)(2,1)S(1)}, bf16[128,512]{1,0:T(8,128)(2,1)S(1)}, u32[]{:S(2)}, u32[]{:S(2)}) %collective-permute-start) | collective-permute-done | bytes 131104 | tf_op jit(solution)/shard_map/while/body/eval_jaxpr/ppermute | solution.py:10
  1178.3 64.9 %collective-permute-done = bf16[128,512]{1,0:T(8,128)(2,1)S(1)} collective-permute-done((bf16[128,512]{1,0:T(8,128)(2,1)S(1)}, bf16[128,512]{1,0:T(8,128)(2,1)S(1)}, u32[]{:S(2)}, u32[]{:S(2)}) %collective-permute-start) | collective-permute-done | bytes 131104 | tf_op jit(solution)/shard_map/while/body/eval_jaxpr/ppermute | solution.py:10
  1358.4 21.7 %collective-permute-done = bf16[128,512]{1,0:T(8,128)(2,1)S(1)} collective-permute-done((bf16[128,512]{1,0:T(8,128)(2,1)S(1)}, bf16[128,512]{1,0:T(8,128)(2,1)S(1)}, u32[]{:S(2)}, u32[]{:S(2)}) %collective-permute-start) | collective-permute-done | bytes 131104 | tf_op jit(solution)/shard_map/while/body/eval_jaxpr/ppermute | solution.py:10
  1389.1 27.8 %collective-permute-done = bf16[128,512]{1,0:T(8,128)(2,1)S(1)} collective-permute-done((bf16[128,512]{1,0:T(8,128)(2,1)S(1)}, bf16[128,512]{1,0:T(8,128)(2,1)S(1)}, u32[]{:S(2)}, u32[]{:S(2)}) %collective-permute-start) | collective-permute-done | bytes 131104 | tf_op jit(solution)/shard_map/while/body/eval_jaxpr/ppermute | solution.py:10
  1428.6 31.5 %collective-permute-done = bf16[128,512]{1,0:T(8,128)(2,1)S(1)} collective-permute-done((bf16[128,512]{1,0:T(8,128)(2,1)S(1)}, bf16[128,512]{1,0:T(8,128)(2,1)S(1)}, u32[]{:S(2)}, u32[]{:S(2)}) %collective-permute-start) | collective-permute-done | bytes 131104 | tf_op jit(solution)/shard_map/while/body/eval_jaxpr/ppermute | solution.py:10
  1471.8 39.5 %collective-permute-done = bf16[128,512]{1,0:T(8,128)(2,1)S(1)} collective-permute-done((bf16[128,512]{1,0:T(8,128)(2,1)S(1)}, bf16[128,512]{1,0:T(8,128)(2,1)S(1)}, u32[]{:S(2)}, u32[]{:S(2)}) %collective-permute-start) | collective-permute-done | bytes 131104 | tf_op jit(solution)/shard_map/while/body/eval_jaxpr/ppermute | solution.py:10
  1555.9 39.9 %collective-permute-done = bf16[128,512]{1,0:T(8,128)(2,1)S(1)} collective-permute-done((bf16[128,512]{1,0:T(8,128)(2,1)S(1)}, bf16[128,512]{1,0:T(8,128)(2,1)S(1)}, u32[]{:S(2)}, u32[]{:S(2)}) %collective-permute-start) | collective-permute-done | bytes 131104 | tf_op jit(solution)/shard_map/while/body/eval_jaxpr/ppermute | solution.py:10
  1607.5 35.6 %collective-permute-done = bf16[128,512]{1,0:T(8,128)(2,1)S(1)} collective-permute-done((bf16[128,512]{1,0:T(8,128)(2,1)S(1)}, bf16[128,512]{1,0:T(8,128)(2,1)S(1)}, u32[]{:S(2)}, u32[]{:S(2)}) %collective-permute-start) | collective-permute-done | bytes 131104 | tf_op jit(solution)/shard_map/while/body/eval_jaxpr/ppermute | solution.py:10
  1684.4 208.5 %reduce-scatter.2.cloned.1.call-done = bf16[128,512]{1,0:T(8,128)(2,1)} async-done(((bf16[1024,512]{1,0:T(8,128)(2,1)}), bf16[128,512]{1,0:T(8,128)(2,1)}) %reduce-scatter.2.cloned.1.call-update) | async-done | bytes 131088 | tf_op jit(solution)/shard_map/reduce_scatter | solution.py:64
  (368 shorter events, 1010.5 us)
Async XLA Ops:
  9.8 41.5 %all-to-all-start = ((bf16[8,128,512]{2,1,0:T(8,128)(2,1)}), bf16[8,128,512]{2,1,0:T(8,128)(2,1)S(1)}, u32[]{:S(2)}, u32[]{:S(2)}) async-start(bf16[8,128,512]{2,1,0:T(8,128)(2,1)} %stack.2), calls=%async_computation | async-start | bytes 2097152 | tf_op jit(solution)/shard_map/all_to_all | solution.py:21
  22.5 1870.3 %reduce-scatter.2.cloned.1.call-start = ((), (), s32[]{:S(2)}) async-start(), calls=%async_computation.2 | async-start | bytes 1179648 | tf_op jit(solution)/shard_map/reduce_scatter | solution.py:64
  144.0 27.9 %collective-permute-start = (bf16[128,512]{1,0:T(8,128)(2,1)S(1)}, bf16[128,512]{1,0:T(8,128)(2,1)S(1)}, u32[]{:S(2)}, u32[]{:S(2)}) collective-permute-start(bf16[128,512]{1,0:T(8,128)(2,1)S(1)} %get-tuple-element.784), channel_id=1, source_target_pairs={{504,0},{0,8},{8,16},{16,24},{24,32},{32,40},{40,48},{48,56},{56,6... | collective-permute-start | bytes 393224 | tf_op jit(solution)/shard_map/while/body/eval_jaxpr/ppermute | solution.py:10
  183.2 27.4 %collective-permute-start = (bf16[128,512]{1,0:T(8,128)(2,1)S(1)}, bf16[128,512]{1,0:T(8,128)(2,1)S(1)}, u32[]{:S(2)}, u32[]{:S(2)}) collective-permute-start(bf16[128,512]{1,0:T(8,128)(2,1)S(1)} %get-tuple-element.784), channel_id=1, source_target_pairs={{504,0},{0,8},{8,16},{16,24},{24,32},{32,40},{40,48},{48,56},{56,6... | collective-permute-start | bytes 393224 | tf_op jit(solution)/shard_map/while/body/eval_jaxpr/ppermute | solution.py:10
  262.1 22.2 %collective-permute-start = (bf16[128,512]{1,0:T(8,128)(2,1)S(1)}, bf16[128,512]{1,0:T(8,128)(2,1)S(1)}, u32[]{:S(2)}, u32[]{:S(2)}) collective-permute-start(bf16[128,512]{1,0:T(8,128)(2,1)S(1)} %get-tuple-element.784), channel_id=1, source_target_pairs={{504,0},{0,8},{8,16},{16,24},{24,32},{32,40},{40,48},{48,56},{56,6... | collective-permute-start | bytes 393224 | tf_op jit(solution)/shard_map/while/body/eval_jaxpr/ppermute | solution.py:10
  353.0 25.5 %collective-permute-start = (bf16[128,512]{1,0:T(8,128)(2,1)S(1)}, bf16[128,512]{1,0:T(8,128)(2,1)S(1)}, u32[]{:S(2)}, u32[]{:S(2)}) collective-permute-start(bf16[128,512]{1,0:T(8,128)(2,1)S(1)} %get-tuple-element.784), channel_id=1, source_target_pairs={{504,0},{0,8},{8,16},{16,24},{24,32},{32,40},{40,48},{48,56},{56,6... | collective-permute-start | bytes 393224 | tf_op jit(solution)/shard_map/while/body/eval_jaxpr/ppermute | solution.py:10
  403.1 45.9 %collective-permute-start = (bf16[128,512]{1,0:T(8,128)(2,1)S(1)}, bf16[128,512]{1,0:T(8,128)(2,1)S(1)}, u32[]{:S(2)}, u32[]{:S(2)}) collective-permute-start(bf16[128,512]{1,0:T(8,128)(2,1)S(1)} %get-tuple-element.784), channel_id=1, source_target_pairs={{504,0},{0,8},{8,16},{16,24},{24,32},{32,40},{40,48},{48,56},{56,6... | collective-permute-start | bytes 393224 | tf_op jit(solution)/shard_map/while/body/eval_jaxpr/ppermute | solution.py:10
  450.2 30.1 %collective-permute-start = (bf16[128,512]{1,0:T(8,128)(2,1)S(1)}, bf16[128,512]{1,0:T(8,128)(2,1)S(1)}, u32[]{:S(2)}, u32[]{:S(2)}) collective-permute-start(bf16[128,512]{1,0:T(8,128)(2,1)S(1)} %get-tuple-element.784), channel_id=1, source_target_pairs={{504,0},{0,8},{8,16},{16,24},{24,32},{32,40},{40,48},{48,56},{56,6... | collective-permute-start | bytes 393224 | tf_op jit(solution)/shard_map/while/body/eval_jaxpr/ppermute | solution.py:10
  496.9 38.1 %collective-permute-start = (bf16[128,512]{1,0:T(8,128)(2,1)S(1)}, bf16[128,512]{1,0:T(8,128)(2,1)S(1)}, u32[]{:S(2)}, u32[]{:S(2)}) collective-permute-start(bf16[128,512]{1,0:T(8,128)(2,1)S(1)} %get-tuple-element.784), channel_id=1, source_target_pairs={{504,0},{0,8},{8,16},{16,24},{24,32},{32,40},{40,48},{48,56},{56,6... | collective-permute-start | bytes 393224 | tf_op jit(solution)/shard_map/while/body/eval_jaxpr/ppermute | solution.py:10
  606.8 52.8 %collective-permute-start = (bf16[128,512]{1,0:T(8,128)(2,1)S(1)}, bf16[128,512]{1,0:T(8,128)(2,1)S(1)}, u32[]{:S(2)}, u32[]{:S(2)}) collective-permute-start(bf16[128,512]{1,0:T(8,128)(2,1)S(1)} %get-tuple-element.784), channel_id=1, source_target_pairs={{504,0},{0,8},{8,16},{16,24},{24,32},{32,40},{40,48},{48,56},{56,6... | collective-permute-start | bytes 393224 | tf_op jit(solution)/shard_map/while/body/eval_jaxpr/ppermute | solution.py:10
  699.5 54.0 %collective-permute-start = (bf16[128,512]{1,0:T(8,128)(2,1)S(1)}, bf16[128,512]{1,0:T(8,128)(2,1)S(1)}, u32[]{:S(2)}, u32[]{:S(2)}) collective-permute-start(bf16[128,512]{1,0:T(8,128)(2,1)S(1)} %get-tuple-element.784), channel_id=1, source_target_pairs={{504,0},{0,8},{8,16},{16,24},{24,32},{32,40},{40,48},{48,56},{56,6... | collective-permute-start | bytes 393224 | tf_op jit(solution)/shard_map/while/body/eval_jaxpr/ppermute | solution.py:10
  791.0 31.5 %collective-permute-start = (bf16[128,512]{1,0:T(8,128)(2,1)S(1)}, bf16[128,512]{1,0:T(8,128)(2,1)S(1)}, u32[]{:S(2)}, u32[]{:S(2)}) collective-permute-start(bf16[128,512]{1,0:T(8,128)(2,1)S(1)} %get-tuple-element.784), channel_id=1, source_target_pairs={{504,0},{0,8},{8,16},{16,24},{24,32},{32,40},{40,48},{48,56},{56,6... | collective-permute-start | bytes 393224 | tf_op jit(solution)/shard_map/while/body/eval_jaxpr/ppermute | solution.py:10
  833.9 36.9 %collective-permute-start = (bf16[128,512]{1,0:T(8,128)(2,1)S(1)}, bf16[128,512]{1,0:T(8,128)(2,1)S(1)}, u32[]{:S(2)}, u32[]{:S(2)}) collective-permute-start(bf16[128,512]{1,0:T(8,128)(2,1)S(1)} %get-tuple-element.784), channel_id=1, source_target_pairs={{504,0},{0,8},{8,16},{16,24},{24,32},{32,40},{40,48},{48,56},{56,6... | collective-permute-start | bytes 393224 | tf_op jit(solution)/shard_map/while/body/eval_jaxpr/ppermute | solution.py:10
  872.0 22.3 %collective-permute-start = (bf16[128,512]{1,0:T(8,128)(2,1)S(1)}, bf16[128,512]{1,0:T(8,128)(2,1)S(1)}, u32[]{:S(2)}, u32[]{:S(2)}) collective-permute-start(bf16[128,512]{1,0:T(8,128)(2,1)S(1)} %get-tuple-element.784), channel_id=1, source_target_pairs={{504,0},{0,8},{8,16},{16,24},{24,32},{32,40},{40,48},{48,56},{56,6... | collective-permute-start | bytes 393224 | tf_op jit(solution)/shard_map/while/body/eval_jaxpr/ppermute | solution.py:10
  895.5 47.5 %collective-permute-start = (bf16[128,512]{1,0:T(8,128)(2,1)S(1)}, bf16[128,512]{1,0:T(8,128)(2,1)S(1)}, u32[]{:S(2)}, u32[]{:S(2)}) collective-permute-start(bf16[128,512]{1,0:T(8,128)(2,1)S(1)} %get-tuple-element.784), channel_id=1, source_target_pairs={{504,0},{0,8},{8,16},{16,24},{24,32},{32,40},{40,48},{48,56},{56,6... | collective-permute-start | bytes 393224 | tf_op jit(solution)/shard_map/while/body/eval_jaxpr/ppermute | solution.py:10
  944.1 22.2 %collective-permute-start = (bf16[128,512]{1,0:T(8,128)(2,1)S(1)}, bf16[128,512]{1,0:T(8,128)(2,1)S(1)}, u32[]{:S(2)}, u32[]{:S(2)}) collective-permute-start(bf16[128,512]{1,0:T(8,128)(2,1)S(1)} %get-tuple-element.784), channel_id=1, source_target_pairs={{504,0},{0,8},{8,16},{16,24},{24,32},{32,40},{40,48},{48,56},{56,6... | collective-permute-start | bytes 393224 | tf_op jit(solution)/shard_map/while/body/eval_jaxpr/ppermute | solution.py:10
  1096.2 27.7 %collective-permute-start = (bf16[128,512]{1,0:T(8,128)(2,1)S(1)}, bf16[128,512]{1,0:T(8,128)(2,1)S(1)}, u32[]{:S(2)}, u32[]{:S(2)}) collective-permute-start(bf16[128,512]{1,0:T(8,128)(2,1)S(1)} %get-tuple-element.784), channel_id=1, source_target_pairs={{504,0},{0,8},{8,16},{16,24},{24,32},{32,40},{40,48},{48,56},{56,6... | collective-permute-start | bytes 393224 | tf_op jit(solution)/shard_map/while/body/eval_jaxpr/ppermute | solution.py:10
  1175.8 67.5 %collective-permute-start = (bf16[128,512]{1,0:T(8,128)(2,1)S(1)}, bf16[128,512]{1,0:T(8,128)(2,1)S(1)}, u32[]{:S(2)}, u32[]{:S(2)}) collective-permute-start(bf16[128,512]{1,0:T(8,128)(2,1)S(1)} %get-tuple-element.784), channel_id=1, source_target_pairs={{504,0},{0,8},{8,16},{16,24},{24,32},{32,40},{40,48},{48,56},{56,6... | collective-permute-start | bytes 393224 | tf_op jit(solution)/shard_map/while/body/eval_jaxpr/ppermute | solution.py:10
  1355.9 24.2 %collective-permute-start = (bf16[128,512]{1,0:T(8,128)(2,1)S(1)}, bf16[128,512]{1,0:T(8,128)(2,1)S(1)}, u32[]{:S(2)}, u32[]{:S(2)}) collective-permute-start(bf16[128,512]{1,0:T(8,128)(2,1)S(1)} %get-tuple-element.784), channel_id=1, source_target_pairs={{504,0},{0,8},{8,16},{16,24},{24,32},{32,40},{40,48},{48,56},{56,6... | collective-permute-start | bytes 393224 | tf_op jit(solution)/shard_map/while/body/eval_jaxpr/ppermute | solution.py:10
  1381.3 35.7 %collective-permute-start = (bf16[128,512]{1,0:T(8,128)(2,1)S(1)}, bf16[128,512]{1,0:T(8,128)(2,1)S(1)}, u32[]{:S(2)}, u32[]{:S(2)}) collective-permute-start(bf16[128,512]{1,0:T(8,128)(2,1)S(1)} %get-tuple-element.784), channel_id=1, source_target_pairs={{504,0},{0,8},{8,16},{16,24},{24,32},{32,40},{40,48},{48,56},{56,6... | collective-permute-start | bytes 393224 | tf_op jit(solution)/shard_map/while/body/eval_jaxpr/ppermute | solution.py:10
  1426.1 34.1 %collective-permute-start = (bf16[128,512]{1,0:T(8,128)(2,1)S(1)}, bf16[128,512]{1,0:T(8,128)(2,1)S(1)}, u32[]{:S(2)}, u32[]{:S(2)}) collective-permute-start(bf16[128,512]{1,0:T(8,128)(2,1)S(1)} %get-tuple-element.784), channel_id=1, source_target_pairs={{504,0},{0,8},{8,16},{16,24},{24,32},{32,40},{40,48},{48,56},{56,6... | collective-permute-start | bytes 393224 | tf_op jit(solution)/shard_map/while/body/eval_jaxpr/ppermute | solution.py:10
  1469.2 42.0 %collective-permute-start = (bf16[128,512]{1,0:T(8,128)(2,1)S(1)}, bf16[128,512]{1,0:T(8,128)(2,1)S(1)}, u32[]{:S(2)}, u32[]{:S(2)}) collective-permute-start(bf16[128,512]{1,0:T(8,128)(2,1)S(1)} %get-tuple-element.784), channel_id=1, source_target_pairs={{504,0},{0,8},{8,16},{16,24},{24,32},{32,40},{40,48},{48,56},{56,6... | collective-permute-start | bytes 393224 | tf_op jit(solution)/shard_map/while/body/eval_jaxpr/ppermute | solution.py:10
  1553.4 42.4 %collective-permute-start = (bf16[128,512]{1,0:T(8,128)(2,1)S(1)}, bf16[128,512]{1,0:T(8,128)(2,1)S(1)}, u32[]{:S(2)}, u32[]{:S(2)}) collective-permute-start(bf16[128,512]{1,0:T(8,128)(2,1)S(1)} %get-tuple-element.784), channel_id=1, source_target_pairs={{504,0},{0,8},{8,16},{16,24},{24,32},{32,40},{40,48},{48,56},{56,6... | collective-permute-start | bytes 393224 | tf_op jit(solution)/shard_map/while/body/eval_jaxpr/ppermute | solution.py:10
  1604.9 38.1 %collective-permute-start = (bf16[128,512]{1,0:T(8,128)(2,1)S(1)}, bf16[128,512]{1,0:T(8,128)(2,1)S(1)}, u32[]{:S(2)}, u32[]{:S(2)}) collective-permute-start(bf16[128,512]{1,0:T(8,128)(2,1)S(1)} %get-tuple-element.784), channel_id=1, source_target_pairs={{504,0},{0,8},{8,16},{16,24},{24,32},{32,40},{40,48},{48,56},{56,6... | collective-permute-start | bytes 393224 | tf_op jit(solution)/shard_map/while/body/eval_jaxpr/ppermute | solution.py:10
  (47 other events, 831.6 us)
Sparse Core Ops, SparseCore 0:
  1684.5 208.3 reduce-scatter.1
